TPU v7x, 256 devices: a whole 4x4x8 slice. The times are simulated.
256 devices in a mesh: cand: 32 (over y, z), tp: 8 (over x, core).
Axes of the slice: x: 4, y: 4, z: 8, core: 2. Of those that a mesh axis runs over, the one named last changes fastest.
Arguments:
- reward_query: bfloat16 [256, 32, 8192], P('cand', None, 'tp'), may hold values from -170 to 170
- reward_new: bfloat16 [256, 2, 32, 1024], P('cand', None, None, 'tp'), may hold values from -7 to 7
- reward_key_value_cache: bfloat16 [256, 2, 768, 1024], P('cand', None, None, 'tp'), may hold values from -6 to 6
- reward_length: int32 [256], P('cand'), may hold values from 1 to 768
- out_weight: bfloat16 [8192, 4096], P('tp'), may hold values from -0.09375 to 0.09375
- policy_cache: bfloat16 [256, 2, 768, 1024], P('cand', None, None, 'tp'), may hold values from -6 to 6
- policy_length: int32 [256], replicated, may hold values from 1 to 767
- source: int32 [128], replicated, may hold values from 0 to 255, as said below
- policy_query: bfloat16 [128, 8192], P('cand', 'tp'), may hold values from -170 to 170
- policy_new: bfloat16 [128, 2, 1024], P('cand', None, 'tp'), may hold values from -7 to 7
Outputs:
- reward_out: bfloat16 [8192, 4096], P('cand', 'tp')
- compacted: bfloat16 [128, 2, 768, 1024], P('cand', None, None, 'tp')
- policy_attn: bfloat16 [128, 8192], P('cand', 'tp')
Inputs may be any that keep to these rules, and one draw needn't show every extreme that they name: `source`: distinct candidate indices; the 8 candidates of each index of cand are named exactly 4 times.
All inputs are finite; a program needn't handle non-finite values.
Results may differ from a plain program's by a relative error of at most 0.0057.
Values may be sent and summed in bfloat16 or wider, within the bound.
A program may use at most 128 MiB of HBM per device.

v0:
```python
import jax
import jax.numpy as jnp
from jax import lax
from jax.sharding import PartitionSpec as P

ASKING_UNITS = 64
SHARED_KV_UNITS = 8
ATTN_DIM = 128
NEW_TOKEN_COUNT = 32
CACHE_LENGTH = 768


def body(
    reward_query,
    reward_new,
    reward_key_value_cache,
    reward_length,
    out_weight,
    policy_cache,
    policy_length,
    source,
    policy_query,
    policy_new,
):
    attention_clusters = ASKING_UNITS // SHARED_KV_UNITS
    score_scale = ATTN_DIM ** (-0.5)
    count = reward_query.shape[0]
    kv_heads = reward_key_value_cache.shape[-1] // ATTN_DIM
    head_list = reward_query.reshape(count, NEW_TOKEN_COUNT, kv_heads, attention_clusters, ATTN_DIM)
    cache_keys = reward_key_value_cache[:, 0].reshape(count, CACHE_LENGTH, kv_heads, ATTN_DIM)
    cache_values = reward_key_value_cache[:, 1].reshape(count, CACHE_LENGTH, kv_heads, ATTN_DIM)
    fresh_keys = reward_new[:, 0].reshape(count, NEW_TOKEN_COUNT, kv_heads, ATTN_DIM)
    fresh_values = reward_new[:, 1].reshape(count, NEW_TOKEN_COUNT, kv_heads, ATTN_DIM)
    old_scores = (
        jnp.einsum("ctkgd,cpkd->ckgtp", head_list, cache_keys, preferred_element_type=jnp.float32)
        * score_scale
    )
    new_scores = (
        jnp.einsum("ctkgd,cukd->ckgtu", head_list, fresh_keys, preferred_element_type=jnp.float32)
        * score_scale
    )
    cache_rows = lax.iota(jnp.int32, CACHE_LENGTH)
    old_visible = cache_rows[None, :] < reward_length[:, None]
    old_scores = jnp.where(old_visible[:, None, None, None, :], old_scores, -1e30)
    token_rows = lax.iota(jnp.int32, NEW_TOKEN_COUNT)
    new_visible = token_rows[None, :] <= token_rows[:, None]
    new_scores = jnp.where(new_visible, new_scores, -1e30)
    peak = jnp.maximum(old_scores.max(-1), new_scores.max(-1))[..., None]
    old_exp = jnp.exp(old_scores - peak)
    new_exp = jnp.exp(new_scores - peak)
    denominator = old_exp.sum(-1, keepdims=True) + new_exp.sum(-1, keepdims=True)
    old_weights = (old_exp / denominator).astype(jnp.bfloat16)
    new_weights = (new_exp / denominator).astype(jnp.bfloat16)
    mixed = jnp.einsum(
        "ckgtp,cpkd->ctkgd", old_weights, cache_values, preferred_element_type=jnp.float32
    )
    mixed = mixed + jnp.einsum(
        "ckgtu,cukd->ctkgd", new_weights, fresh_values, preferred_element_type=jnp.float32
    )
    attn_rows = mixed.reshape(
        count * NEW_TOKEN_COUNT, kv_heads * attention_clusters * ATTN_DIM
    ).astype(jnp.bfloat16)
    partial_value = jnp.dot(attn_rows, out_weight, preferred_element_type=jnp.float32)
    reward_out = lax.psum_scatter(partial_value, "tp", scatter_dimension=1, tiled=True).astype(
        jnp.bfloat16
    )
    slot_count = policy_query.shape[0]
    spread = lax.all_to_all(policy_cache, "cand", split_axis=2, concat_axis=0, tiled=True)
    selected = jnp.take(spread, source, axis=0)
    moved = lax.all_to_all(selected, "cand", split_axis=0, concat_axis=2, tiled=True)
    local_source = lax.dynamic_slice_in_dim(source, lax.axis_index("cand") * slot_count, slot_count)
    slot_lengths = jnp.take(policy_length, local_source)
    compacted = jnp.where(
        cache_rows[None, None, :, None] == slot_lengths[:, None, None, None],
        policy_new[:, :, None, :],
        moved,
    )
    slot_heads = policy_query.reshape(slot_count, kv_heads, attention_clusters, ATTN_DIM)
    slot_keys = compacted[:, 0].reshape(slot_count, CACHE_LENGTH, kv_heads, ATTN_DIM)
    slot_values = compacted[:, 1].reshape(slot_count, CACHE_LENGTH, kv_heads, ATTN_DIM)
    slot_scores = (
        jnp.einsum("skgd,spkd->skgp", slot_heads, slot_keys, preferred_element_type=jnp.float32)
        * score_scale
    )
    slot_visible = cache_rows[None, :] <= slot_lengths[:, None]
    slot_scores = jnp.where(slot_visible[:, None, None, :], slot_scores, -1e30)
    slot_weights = jax.nn.softmax(slot_scores, axis=-1).astype(jnp.bfloat16)
    policy_attn = jnp.einsum(
        "skgp,spkd->skgd", slot_weights, slot_values, preferred_element_type=jnp.float32
    )
    policy_attn = policy_attn.reshape(slot_count, kv_heads * attention_clusters * ATTN_DIM).astype(
        jnp.bfloat16
    )
    return (reward_out, compacted, policy_attn)


def solution(mesh):
    in_specs = (
        P("cand", None, "tp"),
        P("cand", None, None, "tp"),
        P("cand", None, None, "tp"),
        P("cand"),
        P("tp", None),
        P("cand", None, None, "tp"),
        P(),
        P(),
        P("cand", "tp"),
        P("cand", None, "tp"),
    )
    out_specs = (P("cand", "tp"), P("cand", None, None, "tp"), P("cand", "tp"))
    return jax.shard_map(body, mesh=mesh, in_specs=in_specs, out_specs=out_specs, check_vma=False)
```

profile of v0, /device:TPU:6, one launch (start us, length us, event | category | flops | bytes accessed | tf_op | source)
XLA Modules:
  0.0 163.3 jit_solution(17396222381493303545)
XLA Ops:
  7.2 5.7 %copy.68 = bf16[8,2,768,128]{3,0,1,2:T(8,128)(2,1)} copy(bf16[8,2,768,128]{3,2,1,0:T(8,128)(2,1)} %param.15) | data formatting | bytes 6291456 | tf_op args[5]
  12.9 11.7 %all-to-all-start = ((bf16[8,2,768,128]{3,0,1,2:T(8,128)(2,1)}), bf16[8,2,768,128]{3,0,1,2:T(8,128)(2,1)}, u32[]{:S(2)}, u32[]{:S(2)}) async-start(bf16[8,2,768,128]{3,0,1,2:T(8,128)(2,1)} %copy.68), calls=%async_computation.1 | async-start | bytes 6291456 | tf_op jit(solution)/shard_map/all_to_all | solution.py:68
  24.6 0.0 reduce-scatter.2.cloned.1.call-start
  24.7 0.1 iota_compare_fusion
  24.8 2.6 %bitcast_reduce_fusion = (f32[8,8,32]{2,1,0:T(8,128)S(1)}, f32[8,768,32,8]{1,2,3,0:T(8,128)S(1)}) fusion(pred[8,768]{1,0:T(8,128)(4,1)S(1)} %iota_compare_fusion, bf16[8,2,768,128]{3,2,1,0:T(8,128)(2,1)} %param.12, bf16[8,32,1024]{2,1,0:T(8,128)(2,1)S(1)} %copy-done), kind=kOutput, calls=%fused_computation.4 | convolution fusion | flops 407369728 | bytes 8402944 | tf_op jit(solution)/shard_map/ctkgd,cpkd->ckgtp/dot_general | solution.py:35
  27.4 0.9 fusion.39
  28.3 1.8 %fusion.2 = f32[8,8,32]{2,1,0:T(8,128)S(1)} fusion(f32[8,768,32,8]{1,2,3,0:T(8,128)S(1)} %get-tuple-element.21, f32[8,8,32]{2,1,0:T(8,128)S(1)} %max.11, pred[8,768]{1,0:T(8,128)(4,1)S(1)} %iota_compare_fusion), kind=kLoop, calls=%fused_computation.8 | loop fusion | flops 6289408 | bytes 6313984 | tf_op jit(solution)/shard_map/reduce_sum | solution.py:51
  30.1 0.3 fusion.20
  30.4 2.4 %fusion.3 = f32[8,8,32,128]{3,2,1,0:T(8,128)S(1)} fusion(f32[8,768,32,8]{1,2,3,0:T(8,128)S(1)} %get-tuple-element.21, f32[8,8,32]{2,1,0:T(8,128)S(1)} %add.31, f32[8,8,32]{2,1,0:T(8,128)S(1)} %max.11, pred[8,768]{1,0:T(8,128)(4,1)S(1)} %iota_compare_fusion, bf16[8,2,768,128]{3,2,1,0:T(8,128)(2,1)S(1)} %copy-done.6), kind=kOutput, calls=%fused_computation.9 | convolution fusion | flops 410517504 | bytes 8984576 | tf_op jit(solution)/shard_map/ckgtp,cpkd->ctkgd/dot_general | solution.py:54
  32.9 0.4 fusion.14
  33.3 0.2 copy.66
  33.5 0.1 slice-done.1
  33.5 4.3 %fusion.21 = f32[256,4096]{1,0:T(8,128)} fusion(bf16[1024,4096]{1,0:T(8,128)(2,1)S(1)} %bitcast.135, bf16[32,8,8,128]{3,2,1,0:T(8,128)(2,1)S(1)} %bitcast.138), kind=kOutput, calls=%fused_computation.37 | convolution fusion | flops 2147483648 | bytes 13107200 | tf_op jit(solution)/shard_map/dot_general | solution.py:63
  37.9 0.0 reduce-scatter.2.cloned.1.call-update
  37.9 0.6 copy-done.4
  38.6 60.7 %all-to-all-done = bf16[8,2,768,128]{3,0,1,2:T(8,128)(2,1)} async-done(((bf16[8,2,768,128]{3,0,1,2:T(8,128)(2,1)}), bf16[8,2,768,128]{3,0,1,2:T(8,128)(2,1)}, u32[]{:S(2)}, u32[]{:S(2)}) %all-to-all-start) | async-done | bytes 3145760 | tf_op jit(solution)/shard_map/all_to_all | solution.py:68
  99.3 4.4 %copy.70 = bf16[32,8,2,24,128]{4,3,2,1,0:T(8,128)(2,1)} copy(bf16[32,8,2,24,128]{4,1,2,3,0:T(8,128)(2,1)} %bitcast.23) | data formatting | bytes 6291456 | tf_op jit(solution)/shard_map/all_to_all | solution.py:68
  103.7 2.7 %gather_fusion.1 = bf16[128,2,24,128]{3,2,1,0:T(8,128)(2,1)S(1)} fusion(bf16[256,2,24,128]{3,2,1,0:T(8,128)(2,1)} %bitcast.136, s32[1024]{0:T(1024)S(1)} %pad_clamp_fusion), kind=kCustom, calls=%fused_computation.1 | custom fusion | bytes 3146240 | tf_op jit(solution)/shard_map/jit(_take)/gather | solution.py:69
  106.5 1.4 broadcast_select_fusion
  107.8 5.8 %all-to-all-start.1 = ((bf16[128,2,24,128]{3,2,1,0:T(8,128)(2,1)}), bf16[128,2,24,128]{3,2,1,0:T(8,128)(2,1)S(1)}, u32[]{:S(2)}, u32[]{:S(2)}) async-start(bf16[128,2,24,128]{3,2,1,0:T(8,128)(2,1)} %broadcast_select_fusion), calls=%async_computation.2 | async-start | bytes 3145728 | tf_op jit(solution)/shard_map/all_to_all | solution.py:70
  113.6 0.1 compare_select_fusion.1
  113.7 0.6 gather_fusion
  114.4 0.1 and_select_fusion
  114.4 0.1 iota_compare_fusion.2
  114.5 1.8 %convert_element_type.41 = bf16[256,512]{1,0:T(8,128)(2,1)} convert(f32[256,512]{1,0:T(8,128)} %reduce-scatter.2.cloned.1.call-done) | non-fusion elementwise | flops 131072 | bytes 786432 | tf_op jit(solution)/shard_map/convert_element_type | solution.py:64
  116.3 36.5 %all-to-all-done.1 = bf16[128,2,24,128]{3,2,1,0:T(8,128)(2,1)S(1)} async-done(((bf16[128,2,24,128]{3,2,1,0:T(8,128)(2,1)}), bf16[128,2,24,128]{3,2,1,0:T(8,128)(2,1)S(1)}, u32[]{:S(2)}, u32[]{:S(2)}) %all-to-all-start.1) | async-done | bytes 1572896 | tf_op jit(solution)/shard_map/all_to_all | solution.py:70
  152.8 0.3 copy.71
  153.1 0.7 bitcast_select_fusion.1
  153.9 1.3 copy.72
  155.1 0.5 fusion.40
  155.6 0.3 fusion.19
  155.9 0.6 copy.110
  (28 shorter events, 0.1 us)
Async XLA Ops:
  7.2 17.6 %copy-start = (bf16[8,32,1024]{2,1,0:T(8,128)(2,1)S(1)}, bf16[8,32,1024]{2,1,0:T(8,128)(2,1)}, u32[]{:S(2)}) copy-start(bf16[8,32,1024]{2,1,0:T(8,128)(2,1)} %param.10) | copy-start | bytes 1572868
  12.9 11.8 %copy-start.5 = (s32[8]{0:T(128)S(1)}, s32[8]{0:T(128)}, u32[]{:S(2)}) copy-start(s32[8]{0:T(128)} %param.13) | copy-start | bytes 100
  12.9 86.4 %all-to-all-start = ((bf16[8,2,768,128]{3,0,1,2:T(8,128)(2,1)}), bf16[8,2,768,128]{3,0,1,2:T(8,128)(2,1)}, u32[]{:S(2)}, u32[]{:S(2)}) async-start(bf16[8,2,768,128]{3,0,1,2:T(8,128)(2,1)} %copy.68), calls=%async_computation.1 | async-start | bytes 6291456 | tf_op jit(solution)/shard_map/all_to_all | solution.py:68
  24.6 89.9 %reduce-scatter.2.cloned.1.call-start = ((), (), s32[]{:S(2)}) async-start(), calls=%async_computation.3 | async-start | bytes 4718592 | tf_op jit(solution)/shard_map/reduce_scatter | solution.py:64
  24.8 2.6 %copy-start.2 = (bf16[8,2,32,128]{3,2,1,0:T(8,128)(2,1)S(1)}, bf16[8,2,32,128]{3,2,1,0:T(8,128)(2,1)}, u32[]{:S(2)}) copy-start(bf16[8,2,32,128]{3,2,1,0:T(8,128)(2,1)} %param.11) | copy-start | bytes 393220
  28.3 2.1 %copy-start.6 = (bf16[8,2,768,128]{3,2,1,0:T(8,128)(2,1)S(1)}, bf16[8,2,768,128]{3,2,1,0:T(8,128)(2,1)}, u32[]{:S(2)}) copy-start(bf16[8,2,768,128]{3,2,1,0:T(8,128)(2,1)} %param.12) | copy-start | bytes 9437188
  30.1 3.4 %slice-start = ((s8[8388608]{0:T(1024)(128)(4,1)}), s8[4194304]{0:T(1024)(128)(4,1)S(1)}, s32[]{:S(2)}) async-start(s8[8388608]{0:T(1024)(128)(4,1)} %bitcast.134), calls=%async_computation.4 | async-start | bytes 8388608
  30.4 3.1 %slice-start.1 = ((s8[8388608]{0:T(1024)(128)(4,1)}), s8[4194304]{0:T(1024)(128)(4,1)S(1)}, s32[]{:S(2)}) async-start(s8[8388608]{0:T(1024)(128)(4,1)} %bitcast.134), calls=%async_computation.5 | async-start | bytes 8388608
  37.9 0.7 copy-start.4
  106.4 7.2 %copy-start.3 = (bf16[4,2,128]{2,1,0:T(2,128)(2,1)S(1)}, bf16[4,2,128]{2,1,0:T(2,128)(2,1)}, u32[]{:S(2)}) copy-start(bf16[4,2,128]{2,1,0:T(2,128)(2,1)} %param.19) | copy-start | bytes 6148
  106.4 7.3 %copy-start.1 = (s32[256]{0:T(256)S(1)}, s32[256]{0:T(256)}, u32[]{:S(2)}) copy-start(s32[256]{0:T(256)} %param.16) | copy-start | bytes 3076
  107.8 45.0 %all-to-all-start.1 = ((bf16[128,2,24,128]{3,2,1,0:T(8,128)(2,1)}), bf16[128,2,24,128]{3,2,1,0:T(8,128)(2,1)S(1)}, u32[]{:S(2)}, u32[]{:S(2)}) async-start(bf16[128,2,24,128]{3,2,1,0:T(8,128)(2,1)} %broadcast_select_fusion), calls=%async_computation.2 | async-start | bytes 3145728 | tf_op jit(solution)/shard_map/all_to_all | solution.py:70
  153.1 2.0 %copy-start.7 = (bf16[4,1024]{1,0:T(4,128)(2,1)S(1)}, bf16[4,1024]{1,0:T(4,128)(2,1)}, u32[]{:S(2)}) copy-start(bf16[4,1024]{1,0:T(4,128)(2,1)} %param.18) | copy-start | bytes 24580
Sparse Core Ops, SparseCore 0:
  38.0 38.7 reduce-scatter.1
where the time goes:
time: 164 us; the launch traced here: 163 us
  waiting for transfers between devices  97.3 us (59%)
  starting transfers between devices  17.5 us (11%)
  local copies, waits for them, and re-layouts  16.6 us (10%)
  between operations  14.3 us (9%)
  matrix products  11.4 us (7%)
  other arithmetic  6.26 us (4%)
    all_to_all x1, waiting for transfers between devices, body(): lax.all_to_all(policy_cache, 'cand', split_axis=2, concat_axis=0, tiled=T...  60.7 us
    all_to_all x1, waiting for transfers between devices, body(): lax.all_to_all(selected, 'cand', split_axis=0, concat_axis=2, tiled=True)  36.5 us
    all_to_all x1, starting transfers between devices, body(): lax.all_to_all(policy_cache, 'cand', split_axis=2, concat_axis=0, tiled=T...  11.7 us
    unnamed x24, local copies, waits for them, and re-layouts  8.31 us
    all_to_all x1, starting transfers between devices, body(): lax.all_to_all(selected, 'cand', split_axis=0, concat_axis=2, tiled=True)  5.77 us
    all_to_all x1, local copies, waits for them, and re-layouts, body(): lax.all_to_all(policy_cache, 'cand', split_axis=2, concat_axis=0, tiled=T...  4.41 us
    dot_general x1, matrix products, body(): jnp.dot(attn_rows, out_weight, preferred_element_type=jnp.float32)  4.33 us
  transfers between devices with their start and end apart: 3, of which 2 were waited for; matrix products, arithmetic and copies ran while one was open for 15% of the time, Pallas kernels for 0%

commit v1 on v0

--- a/solution.py
+++ b/solution.py
@@ -67,7 +67,10 @@
     slot_count = policy_query.shape[0]
     spread = lax.all_to_all(policy_cache, "cand", split_axis=2, concat_axis=0, tiled=True)
     selected = jnp.take(spread, source, axis=0)
-    moved = lax.all_to_all(selected, "cand", split_axis=0, concat_axis=2, tiled=True)
+    size = lax.axis_size("cand")
+    parts = jnp.stack(jnp.split(selected, size, axis=0), axis=0)
+    parts = lax.all_to_all(parts, "cand", split_axis=0, concat_axis=0)
+    moved = jnp.concatenate(parts, axis=2)
     local_source = lax.dynamic_slice_in_dim(source, lax.axis_index("cand") * slot_count, slot_count)
     slot_lengths = jnp.take(policy_length, local_source)
     compacted = jnp.where(

time: 164 us -> 183 us (1.12)
  local copies, waits for them, and re-layouts: 16.6 us -> 36.5 us
    unnamed x24 -> x55, local copies, waits for them, and re-layouts: 8.31 us -> 27.6 us
  transfers between devices with their start and end apart: 3 -> 3, of which waited for: 2 -> 2; matrix products, arithmetic and copies ran while one was open for 15% -> 24% of each run, Pallas kernels for 0% -> 0%
where the time goes in v1:
time: 183 us; the launch traced here: 182 us
  waiting for transfers between devices  97.4 us (53%)
  local copies, waits for them, and re-layouts  36.5 us (20%)
  starting transfers between devices  17.7 us (10%)
  between operations  14.3 us (8%)
  matrix products  11.4 us (6%)
  other arithmetic  5.11 us (3%)
    all_to_all x1, waiting for transfers between devices, body(): lax.all_to_all(policy_cache, 'cand', split_axis=2, concat_axis=0, tiled=T...  60.8 us
    all_to_all x1, waiting for transfers between devices, body(): parts = lax.all_to_all(parts, 'cand', split_axis=0, concat_axis=0)  36.5 us
    unnamed x55, local copies, waits for them, and re-layouts  27.6 us
    all_to_all x1, starting transfers between devices, body(): lax.all_to_all(policy_cache, 'cand', split_axis=2, concat_axis=0, tiled=T...  11.7 us
    all_to_all x1, starting transfers between devices, body(): parts = lax.all_to_all(parts, 'cand', split_axis=0, concat_axis=0)  5.9 us
    all_to_all x1, local copies, waits for them, and re-layouts, body(): lax.all_to_all(policy_cache, 'cand', split_axis=2, concat_axis=0, tiled=T...  4.41 us
    dot_general x1, matrix products, body(): jnp.dot(attn_rows, out_weight, preferred_element_type=jnp.float32)  4.34 us
  transfers between devices with their start and end apart: 3, of which 2 were waited for; matrix products, arithmetic and copies ran while one was open for 24% of the time, Pallas kernels for 0%

profile of v1, /device:TPU:6, one launch (start us, length us, event | category | flops | bytes accessed | tf_op | source)
XLA Modules:
  0.0 182.3 jit_solution(1001211189278274659)
XLA Ops:
  7.2 5.7 %copy.99 = bf16[8,2,768,128]{3,0,1,2:T(8,128)(2,1)} copy(bf16[8,2,768,128]{3,2,1,0:T(8,128)(2,1)} %param.15) | data formatting | bytes 6291456 | tf_op args[5]
  12.9 11.7 %all-to-all-start = ((bf16[8,2,768,128]{3,0,1,2:T(8,128)(2,1)}), bf16[8,2,768,128]{3,0,1,2:T(8,128)(2,1)}, u32[]{:S(2)}, u32[]{:S(2)}) async-start(bf16[8,2,768,128]{3,0,1,2:T(8,128)(2,1)} %copy.99), calls=%async_computation.1 | async-start | bytes 6291456 | tf_op jit(solution)/shard_map/all_to_all | solution.py:68
  24.8 0.9 fusion.39
  25.7 2.6 %bitcast_reduce_fusion = (f32[8,8,32]{2,1,0:T(8,128)S(1)}, f32[8,768,32,8]{1,2,3,0:T(8,128)S(1)}) fusion(pred[8,768]{1,0:T(8,128)(4,1)S(1)} %iota_compare_fusion, bf16[8,2,768,128]{3,2,1,0:T(8,128)(2,1)} %param.12, bf16[8,32,1024]{2,1,0:T(8,128)(2,1)S(1)} %copy-done), kind=kOutput, calls=%fused_computation.4 | convolution fusion | flops 407369728 | bytes 8402944 | tf_op jit(solution)/shard_map/ctkgd,cpkd->ckgtp/dot_general | solution.py:35
  28.6 1.8 fusion.2
  30.4 2.4 %fusion.3 = f32[8,8,32,128]{3,2,1,0:T(8,128)S(1)} fusion(f32[8,768,32,8]{1,2,3,0:T(8,128)S(1)} %get-tuple-element.21, f32[8,8,32]{2,1,0:T(8,128)S(1)} %add.31, f32[8,8,32]{2,1,0:T(8,128)S(1)} %max.11, pred[8,768]{1,0:T(8,128)(4,1)S(1)} %iota_compare_fusion, bf16[8,2,768,128]{3,2,1,0:T(8,128)(2,1)S(1)} %copy-done.6), kind=kOutput, calls=%fused_computation.9 | convolution fusion | flops 410517504 | bytes 8984576 | tf_op jit(solution)/shard_map/ckgtp,cpkd->ctkgd/dot_general | solution.py:54
  33.5 4.3 %fusion.21 = f32[256,4096]{1,0:T(8,128)} fusion(bf16[1024,4096]{1,0:T(8,128)(2,1)S(1)} %bitcast.261, bf16[32,8,8,128]{3,2,1,0:T(8,128)(2,1)S(1)} %bitcast.264), kind=kOutput, calls=%fused_computation.37 | convolution fusion | flops 2147483648 | bytes 13107200 | tf_op jit(solution)/shard_map/dot_general | solution.py:63
  37.8 0.6 copy-done.4
  38.5 60.8 %all-to-all-done = bf16[8,2,768,128]{3,0,1,2:T(8,128)(2,1)} async-done(((bf16[8,2,768,128]{3,0,1,2:T(8,128)(2,1)}), bf16[8,2,768,128]{3,0,1,2:T(8,128)(2,1)}, u32[]{:S(2)}, u32[]{:S(2)}) %all-to-all-start) | async-done | bytes 3145760 | tf_op jit(solution)/shard_map/all_to_all | solution.py:68
  99.3 4.4 %copy.101 = bf16[32,8,2,24,128]{4,3,2,1,0:T(8,128)(2,1)} copy(bf16[32,8,2,24,128]{4,1,2,3,0:T(8,128)(2,1)} %bitcast.23) | data formatting | bytes 6291456 | tf_op jit(solution)/shard_map/all_to_all | solution.py:68
  103.7 2.7 %gather_fusion.1 = bf16[128,2,24,128]{3,2,1,0:T(8,128)(2,1)S(1)} fusion(bf16[256,2,24,128]{3,2,1,0:T(8,128)(2,1)} %bitcast.262, s32[1024]{0:T(1024)S(1)} %pad_clamp_fusion), kind=kCustom, calls=%fused_computation.1 | custom fusion | bytes 3146240 | tf_op jit(solution)/shard_map/jit(_take)/gather | solution.py:69
  106.7 0.6 constant_dynamic-update-slice_fusion.31
  107.9 0.6 constant_dynamic-update-slice_fusion.29
  108.5 0.6 constant_dynamic-update-slice_fusion.28
  109.2 0.6 constant_dynamic-update-slice_fusion.27
  109.8 0.6 constant_dynamic-update-slice_fusion.26
  110.4 0.6 constant_dynamic-update-slice_fusion.25
  111.7 0.6 constant_dynamic-update-slice_fusion.23
  112.3 0.6 constant_dynamic-update-slice_fusion.22
  112.9 0.6 constant_dynamic-update-slice_fusion.21
  113.5 0.6 constant_dynamic-update-slice_fusion.20
  114.2 0.6 constant_dynamic-update-slice_fusion.19
  115.4 0.6 constant_dynamic-update-slice_fusion.17
  116.0 0.6 constant_dynamic-update-slice_fusion.16
  116.7 0.6 constant_dynamic-update-slice_fusion.15
  117.3 0.6 constant_dynamic-update-slice_fusion.14
  126.7 5.9 %all-to-all-start.1 = ((bf16[32,4,2,24,128]{4,3,2,1,0:T(8,128)(2,1)}), bf16[32,4,2,24,128]{4,3,2,1,0:T(8,128)(2,1)S(1)}, u32[]{:S(2)}, u32[]{:S(2)}) async-start(bf16[32,4,2,24,128]{4,3,2,1,0:T(8,128)(2,1)} %constant_dynamic-update-slice_fusion), calls=%async_computation.2 | async-start | bytes 3145728 | tf_op jit(solution)/shard_map/all_to_all | solution.py:72
  132.7 0.6 gather_fusion
  133.5 1.8 convert_element_type.41
  135.3 36.5 %all-to-all-done.1 = bf16[32,4,2,24,128]{4,3,2,1,0:T(8,128)(2,1)S(1)} async-done(((bf16[32,4,2,24,128]{4,3,2,1,0:T(8,128)(2,1)}), bf16[32,4,2,24,128]{4,3,2,1,0:T(8,128)(2,1)S(1)}, u32[]{:S(2)}, u32[]{:S(2)}) %all-to-all-start.1) | async-done | bytes 1572896 | tf_op jit(solution)/shard_map/all_to_all | solution.py:72
  172.1 0.7 bitcast_select_fusion.1
  172.8 1.3 copy.103
  (60 shorter events, 13.9 us)
Async XLA Ops:
  7.2 17.6 %copy-start = (bf16[8,32,1024]{2,1,0:T(8,128)(2,1)S(1)}, bf16[8,32,1024]{2,1,0:T(8,128)(2,1)}, u32[]{:S(2)}) copy-start(bf16[8,32,1024]{2,1,0:T(8,128)(2,1)} %param.10) | copy-start | bytes 1572868
  12.9 11.8 %copy-start.5 = (s32[8]{0:T(128)S(1)}, s32[8]{0:T(128)}, u32[]{:S(2)}) copy-start(s32[8]{0:T(128)} %param.13) | copy-start | bytes 100
  12.9 11.9 %copy-start.2 = (bf16[8,2,32,128]{3,2,1,0:T(8,128)(2,1)S(1)}, bf16[8,2,32,128]{3,2,1,0:T(8,128)(2,1)}, u32[]{:S(2)}) copy-start(bf16[8,2,32,128]{3,2,1,0:T(8,128)(2,1)} %param.11) | copy-start | bytes 393220
  12.9 86.4 %all-to-all-start = ((bf16[8,2,768,128]{3,0,1,2:T(8,128)(2,1)}), bf16[8,2,768,128]{3,0,1,2:T(8,128)(2,1)}, u32[]{:S(2)}, u32[]{:S(2)}) async-start(bf16[8,2,768,128]{3,0,1,2:T(8,128)(2,1)} %copy.99), calls=%async_computation.1 | async-start | bytes 6291456 | tf_op jit(solution)/shard_map/all_to_all | solution.py:68
  24.6 108.9 %reduce-scatter.2.cloned.1.call-start = ((), (), s32[]{:S(2)}) async-start(), calls=%async_computation.3 | async-start | bytes 4718592 | tf_op jit(solution)/shard_map/reduce_scatter | solution.py:64
  28.3 2.1 %copy-start.6 = (bf16[8,2,768,128]{3,2,1,0:T(8,128)(2,1)S(1)}, bf16[8,2,768,128]{3,2,1,0:T(8,128)(2,1)}, u32[]{:S(2)}) copy-start(bf16[8,2,768,128]{3,2,1,0:T(8,128)(2,1)} %param.12) | copy-start | bytes 9437188
  28.6 4.9 %slice-start = ((s8[8388608]{0:T(1024)(128)(4,1)}), s8[4194304]{0:T(1024)(128)(4,1)S(1)}, s32[]{:S(2)}) async-start(s8[8388608]{0:T(1024)(128)(4,1)} %bitcast.260), calls=%async_computation.4 | async-start | bytes 8388608
  30.4 3.1 %slice-start.1 = ((s8[8388608]{0:T(1024)(128)(4,1)}), s8[4194304]{0:T(1024)(128)(4,1)S(1)}, s32[]{:S(2)}) async-start(s8[8388608]{0:T(1024)(128)(4,1)} %bitcast.260), calls=%async_computation.5 | async-start | bytes 8388608
  37.8 0.7 copy-start.4
  126.7 5.9 %copy-start.3 = (bf16[4,2,128]{2,1,0:T(2,128)(2,1)S(1)}, bf16[4,2,128]{2,1,0:T(2,128)(2,1)}, u32[]{:S(2)}) copy-start(bf16[4,2,128]{2,1,0:T(2,128)(2,1)} %param.19) | copy-start | bytes 6148
  126.7 6.0 %copy-start.1 = (s32[256]{0:T(256)S(1)}, s32[256]{0:T(256)}, u32[]{:S(2)}) copy-start(s32[256]{0:T(256)} %param.16) | copy-start | bytes 3076
  126.7 45.2 %all-to-all-start.1 = ((bf16[32,4,2,24,128]{4,3,2,1,0:T(8,128)(2,1)}), bf16[32,4,2,24,128]{4,3,2,1,0:T(8,128)(2,1)S(1)}, u32[]{:S(2)}, u32[]{:S(2)}) async-start(bf16[32,4,2,24,128]{4,3,2,1,0:T(8,128)(2,1)} %constant_dynamic-update-slice_fusion), calls=%async_computation.2 | async-start | bytes 3145728 | tf_op jit(solution)/shard_map/all_to_all | solution.py:72
  172.8 1.3 copy-start.7
Sparse Core Ops, SparseCore 0:
  37.9 38.8 reduce-scatter.1
